TPU v7x, 512 devices: a whole 4x4x16 slice. The times are simulated.
512 devices in a mesh: row: 32 (over z, y_lo), col: 16 (over y_hi, x, core).
Axes of the slice: x: 4, y: 4 (y_hi: 2, y_lo: 2; y = y_hi * 2 + y_lo), z: 16, core: 2. Of those that a mesh axis runs over, the one named last changes fastest.
Arguments:
- coords: int32 [3, 65536], P(None, ('row', 'col')), may hold values from 0 to 60809, as said below
- mode_shapes: bfloat16 [256, 65536], P(None, ('row', 'col')), as said below
- output_shapes: bfloat16 [1048576, 256], P(('row', 'col')), may hold values from -0.375 to 0.375
- response_gain: float32 [2, 256], replicated, may hold values from -4 to 4
Outputs:
- response_power: float32 [1048576], P(('row', 'col'))
- modal_csd: float32 [256, 256], replicated
Inputs may be any that keep to these rules, and one draw needn't show every extreme that they name: `coords`: positions of points on an aircraft's skin, numbered in no spatial order. `mode_shapes`: entries are of order 1 / sqrt(65536); each mode has a share of one sign over all nodes.
All inputs are finite; a program needn't handle non-finite values.
Results may differ from a plain program's by a relative error of at most 0.002.
Values may be sent and summed in bfloat16 or wider, within the bound.
A program may use at most 64 MiB of HBM per device.

v0:
```python
import math
import jax
import jax.numpy as jnp
from jax import lax
from jax.sharding import PartitionSpec as P

wave_scale = 0.35 / 64.0


def coherence(left_points, right_points):
    difference = (left_points[:, :, None] - right_points[:, None, :]).astype(jnp.float32)
    squared = jnp.sum(difference * difference, axis=0)
    return jnp.sinc(wave_scale * jnp.sqrt(squared)).astype(jnp.bfloat16)


def split_parts(matrix):
    high_part = matrix.astype(jnp.bfloat16)
    low_part = (matrix - high_part.astype(jnp.float32)).astype(jnp.bfloat16)
    return (high_part, low_part)


def modal_product(node_shapes, node_projection):
    high_part, low_part = split_parts(node_projection)
    dims = (((1,), (1,)), ((), ()))
    upper = lax.dot_general(node_shapes, high_part, dims, preferred_element_type=jnp.float32)
    lower = lax.dot_general(node_shapes, low_part, dims, preferred_element_type=jnp.float32)
    return upper + lower


def local(coords, mode_shapes, output_shapes, response_gain):
    row_shapes, row_points = (
        lax.all_gather(mode_shapes, "col", axis=1, tiled=True),
        lax.all_gather(coords, "col", axis=1, tiled=True),
    )
    mode_count = mode_shapes.shape[0]
    zero_block = jnp.zeros((mode_count, row_points.shape[1]), jnp.float32)
    piece_shapes = lax.all_gather(mode_shapes, "row", axis=1, tiled=True)
    piece_points = lax.all_gather(coords, "row", axis=1, tiled=True)
    length = piece_shapes.shape[1]
    block_size = math.gcd(length, 1024)
    block_count = length // block_size

    def add_block(loop_index, running_sum):
        block_start = loop_index * block_size
        part_shapes = lax.dynamic_slice_in_dim(piece_shapes, block_start, block_size, 1)
        part_points = lax.dynamic_slice_in_dim(piece_points, block_start, block_size, 1)
        coherence_tile = coherence(part_points, row_points)
        return running_sum + jnp.dot(
            part_shapes, coherence_tile, preferred_element_type=jnp.float32
        )

    projection = lax.fori_loop(0, block_count, add_block, zero_block)
    partial_csd = modal_product(row_shapes, projection)
    modal_csd = lax.psum(partial_csd, ("row", "col"))
    real_part = response_gain[0]
    imag_part = response_gain[1]
    weighted = (
        real_part[:, None] * real_part[None, :] + imag_part[:, None] * imag_part[None, :]
    ) * modal_csd
    weighted_high, weighted_low = split_parts(weighted)
    mapped = jnp.dot(output_shapes, weighted_high, preferred_element_type=jnp.float32)
    mapped = mapped + jnp.dot(output_shapes, weighted_low, preferred_element_type=jnp.float32)
    response_power = jnp.sum(mapped * output_shapes.astype(jnp.float32), axis=1)
    return (response_power, modal_csd)


def solution(mesh):
    in_specs = (P(None, ("row", "col")), P(None, ("row", "col")), P(("row", "col"), None), P())
    out_specs = (P(("row", "col")), P())
    return jax.shard_map(local, mesh=mesh, in_specs=in_specs, out_specs=out_specs, check_vma=False)
```

profile of v0, /device:TPU:4, one launch (start us, length us, event | category | flops | bytes accessed | tf_op | source)
XLA Modules:
  0.0 702.3 jit_solution(17819532380165018910)
XLA Ops:
  7.2 0.0 all-gather.3.cloned.1.call-start
  7.2 0.7 all-gather.3.cloned.1.call-update
  7.9 0.0 all-gather.5.cloned.1.call-start
  7.9 0.7 all-gather.5.cloned.1.call-update
  8.6 0.0 all-reduce.2.cloned.1.call-start
  8.7 69.6 %all_gather.13 = s32[3,4096]{1,0:T(4,128)S(1)} all-gather(s32[3,128]{1,0:T(4,128)} %param.6), channel_id=1, replica_groups=mesh['row'=32,'col'=16] {'row'}, dimensions={1}, use_global_device_ids=true | all-gather | bytes 50688 | tf_op jit(solution)/shard_map/all_gather | solution.py:38
  78.3 19.8 %all_gather.14 = s32[3,2048]{1,0:T(4,128)S(1)} all-gather(s32[3,128]{1,0:T(4,128)} %param.6), channel_id=1, replica_groups=mesh['row'=32,'col'=16] {'col'}, dimensions={1}, use_global_device_ids=true | all-gather | bytes 26112 | tf_op jit(solution)/shard_map/all_gather | solution.py:33
  98.1 2.3 copy.8
  100.4 50.3 %all-gather.3.cloned.1.call-done = bf16[256,4096]{1,0:T(8,128)(2,1)} async-done(((bf16[256,128]{1,0:T(8,128)(2,1)}), bf16[256,4096]{1,0:T(8,128)(2,1)}) %all-gather.3.cloned.1.call-update) | async-done | bytes 2097168 | tf_op jit(solution)/shard_map/all_gather | solution.py:37
  150.7 0.0 copy-start.1
  150.7 81.9 %while.16 = (s32[]{:T(128)}, f32[256,2048]{1,0:T(8,128)S(1)}, bf16[256,4096]{1,0:T(8,128)(2,1)}, s32[3,4096]{1,0:T(4,128)S(1)}, s32[3,2048]{1,0:T(4,128)S(1)}, /*index=5*/s32[]{:T(128)}, s32[]{:T(128)}, s32[]{:T(128)}, s32[]{:T(128)}) while((s32[]{:T(128)}, f32[256,2048]{1,0:T(8,128)S(1)}, bf16[256,4096]{1,0:T(8,128)(2,1)}, ...), condition=%wide.region_2.3_spmd.clone, body=%wide.region_0.2_spmd.clone.sunk | while | flops 1171259392 | bytes 21557404 | solution.py:52
  150.7 6.3 multiply_reduce_fusion.2
  157.0 14.1 %fusion.60 = f32[256,2048]{1,0:T(8,128)S(1)} fusion(f32[1024,2048]{1,0:T(8,128)} %multiply_reduce_fusion.2, f32[256,2048]{1,0:T(8,128)S(1)} %get-tuple-element.211, pred[]{:T(512)S(6)} %compare.3, bf16[256,4096]{1,0:T(8,128)(2,1)} %get-tuple-element.221, s32[]{:T(128)S(6)} %select_n.137), kind=kOutput, calls=%fused_computation.26.clone.1 | convolution fusion | flops 1148190720 | bytes 13107205 | tf_op jit(solution)/shard_map/while/body/eval_jaxpr/dot_general | solution.py:48
  171.2 6.3 multiply_reduce_fusion.2
  177.5 14.1 %fusion.60 = f32[256,2048]{1,0:T(8,128)S(1)} fusion(f32[1024,2048]{1,0:T(8,128)} %multiply_reduce_fusion.2, f32[256,2048]{1,0:T(8,128)S(1)} %get-tuple-element.211, pred[]{:T(512)S(6)} %compare.3, bf16[256,4096]{1,0:T(8,128)(2,1)} %get-tuple-element.221, s32[]{:T(128)S(6)} %select_n.137), kind=kOutput, calls=%fused_computation.26.clone.1 | convolution fusion | flops 1148190720 | bytes 13107205 | tf_op jit(solution)/shard_map/while/body/eval_jaxpr/dot_general | solution.py:48
  191.7 6.3 multiply_reduce_fusion.2
  198.0 14.1 %fusion.60 = f32[256,2048]{1,0:T(8,128)S(1)} fusion(f32[1024,2048]{1,0:T(8,128)} %multiply_reduce_fusion.2, f32[256,2048]{1,0:T(8,128)S(1)} %get-tuple-element.211, pred[]{:T(512)S(6)} %compare.3, bf16[256,4096]{1,0:T(8,128)(2,1)} %get-tuple-element.221, s32[]{:T(128)S(6)} %select_n.137), kind=kOutput, calls=%fused_computation.26.clone.1 | convolution fusion | flops 1148190720 | bytes 13107205 | tf_op jit(solution)/shard_map/while/body/eval_jaxpr/dot_general | solution.py:48
  212.1 6.3 multiply_reduce_fusion.2
  218.5 14.1 %fusion.60 = f32[256,2048]{1,0:T(8,128)S(1)} fusion(f32[1024,2048]{1,0:T(8,128)} %multiply_reduce_fusion.2, f32[256,2048]{1,0:T(8,128)S(1)} %get-tuple-element.211, pred[]{:T(512)S(6)} %compare.3, bf16[256,4096]{1,0:T(8,128)(2,1)} %get-tuple-element.221, s32[]{:T(128)S(6)} %select_n.137), kind=kOutput, calls=%fused_computation.26.clone.1 | convolution fusion | flops 1148190720 | bytes 13107205 | tf_op jit(solution)/shard_map/while/body/eval_jaxpr/dot_general | solution.py:48
  232.6 0.0 copy-start
  232.6 0.0 all-gather.5.cloned.1.call-done
  232.6 1.8 fusion.37
  234.4 2.4 fusion.35
  236.8 0.0 all-reduce.2.cloned.1.call-update
  236.9 0.0 copy-done.1
  236.9 453.2 %all-reduce.2.cloned.1.call-done = f32[256,256]{0,1:T(8,128)} async-done(((f32[256,256]{0,1:T(8,128)}), f32[256,256]{0,1:T(8,128)}) %all-reduce.2.cloned.1.call-update) | async-done | bytes 262160 | tf_op jit(solution)/shard_map/psum | solution.py:54
  690.1 1.8 copy.9
  691.9 0.0 copy-done
  691.9 1.4 fusion.40
  693.3 2.5 fusion.34
  (6 shorter events, 0.0 us)
Async XLA Ops:
  7.2 143.5 %all-gather.3.cloned.1.call-start = ((), (), s32[]{:S(2)}) async-start(), calls=%async_computation | async-start | bytes 2162688 | tf_op jit(solution)/shard_map/all_gather | solution.py:37
  7.9 224.7 %all-gather.5.cloned.1.call-start = ((), (), s32[]{:S(2)}) async-start(), calls=%async_computation.1 | async-start | bytes 1114112 | tf_op jit(solution)/shard_map/all_gather | solution.py:32
  8.6 681.4 %all-reduce.2.cloned.1.call-start = ((), (), s32[]{:S(2)}) async-start(), calls=%async_computation.2 | async-start | bytes 524288 | tf_op jit(solution)/shard_map/psum | solution.py:54
  150.7 86.2 %copy-start.1 = (f32[2,256]{1,0:T(2,128)S(1)}, f32[2,256]{1,0:T(2,128)}, u32[]{:S(2)}) copy-start(f32[2,256]{1,0:T(2,128)} %param.9) | copy-start | bytes 6148
  232.6 459.3 %copy-start = (bf16[2048,256]{1,0:T(8,128)(2,1)S(1)}, bf16[2048,256]{1,0:T(8,128)(2,1)}, u32[]{:S(2)}) copy-start(bf16[2048,256]{1,0:T(8,128)(2,1)} %param.8) | copy-start | bytes 3145732
Sparse Core Ops, SparseCore 0:
  10.0 140.6 all-gather.2
  153.8 55.1 all-gather.4
  237.0 453.0 all-reduce.1
where the time goes:
time: 703 us; the launch traced here: 702 us
  waiting for transfers between devices  505 us (72%)
  blocking collectives  89.4 us (13%)
  matrix products  64.5 us (9%)
  other arithmetic  25.3 us (4%)
  between operations  13.8 us (2%)
    psum x1, waiting for transfers between devices, local(): modal_csd = lax.psum(partial_csd, ('row', 'col'))  453 us
    all_gather x1, blocking collectives, local(): piece_points = lax.all_gather(coords, 'row', axis=1, tiled=True)  69.6 us
    dot_general x4, matrix products, add_block(): jnp.dot(part_shapes, coherence_tile, preferred_element_type=jnp.float32)  56.4 us
    all_gather x1, waiting for transfers between devices, local(): piece_shapes = lax.all_gather(mode_shapes, 'row', axis=1, tiled=True)  50.3 us
    reduce_sum x4, other arithmetic, coherence(): squared = jnp.sum(difference * difference, axis=0)  25.3 us
    all_gather x1, blocking collectives, local(): lax.all_gather(coords, 'col', axis=1, tiled=True)  19.8 us
  transfers between devices with their start and end apart: 3, of which 2 were waited for; matrix products, arithmetic and copies ran while one was open for 12% of the time, Pallas kernels for 0%

commit v1 on v0

--- a/solution.py
+++ b/solution.py
@@ -51,7 +51,7 @@
 
     projection = lax.fori_loop(0, block_count, add_block, zero_block)
     partial_csd = modal_product(row_shapes, projection)
-    modal_csd = lax.psum(partial_csd, ("row", "col"))
+    modal_csd = lax.psum(lax.psum(partial_csd, "col"), "row")
     real_part = response_gain[0]
     imag_part = response_gain[1]
     weighted = (

time: 703 us -> 663 us (0.943)
  the two profiles are of different devices: /device:TPU:4 before, /device:TPU:2 now
where the time goes in v1:
time: 663 us
  waiting for transfers between devices  467 us (70%)
  blocking collectives  89.6 us (14%)
  matrix products  64.1 us (10%)
  other arithmetic  25.3 us (4%)
  between operations  13.8 us (2%)
    psum x2, waiting for transfers between devices, local(): modal_csd = lax.psum(lax.psum(partial_csd, 'col'), 'row')  413 us
    all_gather x1, blocking collectives, local(): piece_points = lax.all_gather(coords, 'row', axis=1, tiled=True)  69.6 us
    dot_general x4, matrix products, add_block(): jnp.dot(part_shapes, coherence_tile, preferred_element_type=jnp.float32)  56.4 us
    all_gather x1, waiting for transfers between devices, local(): piece_shapes = lax.all_gather(mode_shapes, 'row', axis=1, tiled=True)  52.6 us
    reduce_sum x4, other arithmetic, coherence(): squared = jnp.sum(difference * difference, axis=0)  25.3 us
    all_gather x1, blocking collectives, local(): lax.all_gather(coords, 'col', axis=1, tiled=True)  20 us
  transfers between devices with their start and end apart: 4, of which 3 were waited for; matrix products, arithmetic and copies ran while one was open for 12% of the time, Pallas kernels for 0%

profile of v1, /device:TPU:2, one launch (start us, length us, event | category | flops | bytes accessed | tf_op | source)
XLA Modules:
  0.0 662.8 jit_solution(7352508061694699674)
XLA Ops:
  7.2 0.0 all-gather.3.cloned.1.call-start
  7.2 0.7 all-gather.3.cloned.1.call-update
  7.9 0.0 all-gather.5.cloned.1.call-start
  7.9 0.7 all-gather.5.cloned.1.call-update
  8.6 0.0 all-reduce.3.cloned.1.call-start
  8.7 69.6 %all_gather.13 = s32[3,4096]{1,0:T(4,128)S(1)} all-gather(s32[3,128]{1,0:T(4,128)} %param.6), channel_id=1, replica_groups=mesh['row'=32,'col'=16] {'row'}, dimensions={1}, use_global_device_ids=true | all-gather | bytes 50688 | tf_op jit(solution)/shard_map/all_gather | solution.py:38
  78.3 20.0 %all_gather.14 = s32[3,2048]{1,0:T(4,128)S(1)} all-gather(s32[3,128]{1,0:T(4,128)} %param.6), channel_id=1, replica_groups=mesh['row'=32,'col'=16] {'col'}, dimensions={1}, use_global_device_ids=true | all-gather | bytes 26112 | tf_op jit(solution)/shard_map/all_gather | solution.py:33
  98.3 52.6 %all-gather.3.cloned.1.call-done = bf16[256,4096]{1,0:T(8,128)(2,1)} async-done(((bf16[256,128]{1,0:T(8,128)(2,1)}), bf16[256,4096]{1,0:T(8,128)(2,1)}) %all-gather.3.cloned.1.call-update) | async-done | bytes 2097168 | tf_op jit(solution)/shard_map/all_gather | solution.py:37
  150.9 0.0 copy-start
  150.9 81.9 %while.16 = (s32[]{:T(128)}, f32[256,2048]{1,0:T(8,128)S(1)}, bf16[256,4096]{1,0:T(8,128)(2,1)}, s32[3,4096]{1,0:T(4,128)S(1)}, s32[3,2048]{1,0:T(4,128)S(1)}, /*index=5*/s32[]{:T(128)}, s32[]{:T(128)}, s32[]{:T(128)}, s32[]{:T(128)}) while((s32[]{:T(128)}, f32[256,2048]{1,0:T(8,128)S(1)}, bf16[256,4096]{1,0:T(8,128)(2,1)}, ...), condition=%wide.region_2.3_spmd.clone, body=%wide.region_0.2_spmd.clone.sunk | while | flops 1171259392 | bytes 21557404 | solution.py:52
  150.9 6.3 multiply_reduce_fusion.2
  157.2 14.1 %fusion.60 = f32[256,2048]{1,0:T(8,128)S(1)} fusion(f32[1024,2048]{1,0:T(8,128)} %multiply_reduce_fusion.2, f32[256,2048]{1,0:T(8,128)S(1)} %get-tuple-element.211, pred[]{:T(512)S(6)} %compare.3, bf16[256,4096]{1,0:T(8,128)(2,1)} %get-tuple-element.221, s32[]{:T(128)S(6)} %select_n.137), kind=kOutput, calls=%fused_computation.26.clone.1 | convolution fusion | flops 1148190720 | bytes 13107205 | tf_op jit(solution)/shard_map/while/body/eval_jaxpr/dot_general | solution.py:48
  171.4 6.3 multiply_reduce_fusion.2
  177.7 14.1 %fusion.60 = f32[256,2048]{1,0:T(8,128)S(1)} fusion(f32[1024,2048]{1,0:T(8,128)} %multiply_reduce_fusion.2, f32[256,2048]{1,0:T(8,128)S(1)} %get-tuple-element.211, pred[]{:T(512)S(6)} %compare.3, bf16[256,4096]{1,0:T(8,128)(2,1)} %get-tuple-element.221, s32[]{:T(128)S(6)} %select_n.137), kind=kOutput, calls=%fused_computation.26.clone.1 | convolution fusion | flops 1148190720 | bytes 13107205 | tf_op jit(solution)/shard_map/while/body/eval_jaxpr/dot_general | solution.py:48
  191.9 6.3 multiply_reduce_fusion.2
  198.2 14.1 %fusion.60 = f32[256,2048]{1,0:T(8,128)S(1)} fusion(f32[1024,2048]{1,0:T(8,128)} %multiply_reduce_fusion.2, f32[256,2048]{1,0:T(8,128)S(1)} %get-tuple-element.211, pred[]{:T(512)S(6)} %compare.3, bf16[256,4096]{1,0:T(8,128)(2,1)} %get-tuple-element.221, s32[]{:T(128)S(6)} %select_n.137), kind=kOutput, calls=%fused_computation.26.clone.1 | convolution fusion | flops 1148190720 | bytes 13107205 | tf_op jit(solution)/shard_map/while/body/eval_jaxpr/dot_general | solution.py:48
  212.4 6.3 multiply_reduce_fusion.2
  218.7 14.1 %fusion.60 = f32[256,2048]{1,0:T(8,128)S(1)} fusion(f32[1024,2048]{1,0:T(8,128)} %multiply_reduce_fusion.2, f32[256,2048]{1,0:T(8,128)S(1)} %get-tuple-element.211, pred[]{:T(512)S(6)} %compare.3, bf16[256,4096]{1,0:T(8,128)(2,1)} %get-tuple-element.221, s32[]{:T(128)S(6)} %select_n.137), kind=kOutput, calls=%fused_computation.26.clone.1 | convolution fusion | flops 1148190720 | bytes 13107205 | tf_op jit(solution)/shard_map/while/body/eval_jaxpr/dot_general | solution.py:48
  232.8 0.0 copy-start.1
  232.8 0.0 all-gather.5.cloned.1.call-done
  232.9 1.7 fusion.37
  234.6 2.4 fusion.35
  237.0 0.0 all-reduce.3.cloned.1.call-update
  237.0 0.0 all-reduce.5.cloned.1.call-start
  237.0 144.8 %all-reduce.3.cloned.1.call-done = f32[256,256]{0,1:T(8,128)} async-done(((f32[256,256]{0,1:T(8,128)}), f32[256,256]{0,1:T(8,128)}) %all-reduce.3.cloned.1.call-update) | async-done | bytes 262160 | tf_op jit(solution)/shard_map/psum | solution.py:54
  381.9 0.0 all-reduce.5.cloned.1.call-update
  381.9 0.0 copy-done
  381.9 0.6 copy.8
  382.6 0.0 copy-done.1
  382.6 268.3 %all-reduce.5.cloned.1.call-done = f32[256,256]{0,1:T(8,128)} async-done(((f32[256,256]{0,1:T(8,128)}), f32[256,256]{0,1:T(8,128)}) %all-reduce.5.cloned.1.call-update) | async-done | bytes 262160 | tf_op jit(solution)/shard_map/psum | solution.py:54
  650.9 1.8 copy.9
  652.7 1.4 fusion.40
  654.1 2.1 fusion.34
  (6 shorter events, 0.0 us)
Async XLA Ops:
  7.2 143.7 %all-gather.3.cloned.1.call-start = ((), (), s32[]{:S(2)}) async-start(), calls=%async_computation | async-start | bytes 2162688 | tf_op jit(solution)/shard_map/all_gather | solution.py:37
  7.9 225.0 %all-gather.5.cloned.1.call-start = ((), (), s32[]{:S(2)}) async-start(), calls=%async_computation.1 | async-start | bytes 1114112 | tf_op jit(solution)/shard_map/all_gather | solution.py:32
  8.6 373.2 %all-reduce.3.cloned.1.call-start = ((), (), s32[]{:S(2)}) async-start(), calls=%async_computation.2 | async-start | bytes 524288 | tf_op jit(solution)/shard_map/psum | solution.py:54
  150.9 231.0 %copy-start = (bf16[2048,256]{1,0:T(8,128)(2,1)S(1)}, bf16[2048,256]{1,0:T(8,128)(2,1)}, u32[]{:S(2)}) copy-start(bf16[2048,256]{1,0:T(8,128)(2,1)} %param.8) | copy-start | bytes 3145732
  232.8 149.8 %copy-start.1 = (f32[2,256]{1,0:T(2,128)S(1)}, f32[2,256]{1,0:T(2,128)}, u32[]{:S(2)}) copy-start(f32[2,256]{1,0:T(2,128)} %param.9) | copy-start | bytes 6148
  237.0 413.9 %all-reduce.5.cloned.1.call-start = ((), (), s32[]{:S(2)}) async-start(), calls=%async_computation.3 | async-start | bytes 524288 | tf_op jit(solution)/shard_map/psum | solution.py:54
Sparse Core Ops, SparseCore 0:
  10.0 140.8 all-gather.2
  154.0 56.1 all-gather.4
  237.1 144.7 all-reduce.2
  384.9 265.9 all-reduce.4
